TPU v7x, 32 devices: a whole 2x2x4 slice. The times are simulated.
32 devices in a mesh: groups: 2 (over x), head: 8 (over z, y), tensor: 2 (over core).
Axes of the slice: x: 2, y: 2, z: 4, core: 2. Of those that a mesh axis runs over, the one named last changes fastest.
Arguments:
- query: bfloat16 [8192, 1024], P(('groups', 'head'), 'tensor'), parts along dimension 0, may hold values from -32 to 32
- keys_in: bfloat16 [8192, 1024], P(('groups', 'head'), 'tensor'), parts along dimension 0, may hold values from -6 to 6
- values_in: bfloat16 [8192, 1024], P(('groups', 'head'), 'tensor'), parts along dimension 0, may hold values from -6 to 6
- grad_out: bfloat16 [8192, 1024], P(('groups', 'head'), 'tensor'), parts along dimension 0, may hold values from -96 to 96
- w_out: bfloat16 [1024, 1024], P('tensor'), may hold values from -0.1875 to 0.1875
- w_query: bfloat16 [1024, 1024], P(None, 'tensor'), may hold values from -0.1875 to 0.1875
- w_key: bfloat16 [1024, 1024], P(None, 'tensor'), may hold values from -0.1875 to 0.1875
- w_value: bfloat16 [1024, 1024], P(None, 'tensor'), may hold values from -0.1875 to 0.1875
- perm: int32 [2, 4096], P('groups'), parts along dimension 0, may hold values from 0 to 4095, as said below
- blocks: int32 [2, 32, 12], P('groups'), parts along dimension 0, may hold values from 0 to 31, as said below
- counts: int32 [2, 32], P('groups'), parts along dimension 0, may hold values from 1 to 12
Outputs:
- input_grad: bfloat16 [8192, 1024], P(('groups', 'head', 'tensor')), parts along dimension 0
There are 2 independent parts, one for each index of `groups`. A program takes and returns all parts, laid end to end along the dimension named above; an argument that names none is the same for every part. Nothing has to cross between parts.
Inputs may be any that keep to these rules, and one draw needn't show every extreme that they name: Each row of perm holds every node number of the graph once. blocks[g, b, 0] is b; the 12 entries of blocks[g, b] are different block numbers.
All inputs are finite; a program needn't handle non-finite values.
Results may differ from a plain program's by a relative error of at most 0.011.
Values may be sent and summed in bfloat16 or wider, within the bound.
A program may use at most 64 MiB of HBM per device.

v0:
```python
import jax
import jax.numpy as jnp
from jax import lax
from jax.sharding import PartitionSpec as P

HD = 64
BS = 128
KB = 12


def on_device(
    query, keys_in, values_in, grad_out, w_out, w_query, w_key, w_value, perm, blocks, counts
):
    local_rows, half_width = query.shape
    graph_count, graph_nodes = perm.shape
    half_heads = half_width // HD
    part_rows = local_rows // graph_count
    block_count = graph_nodes // BS
    group_size = 512 // BS
    scale = HD ** (-0.5)
    attn_grad = lax.dot_general(
        lax.all_gather(grad_out, "tensor", axis=1, tiled=True),
        w_out,
        (((1,), (1,)), ((), ())),
        preferred_element_type=jnp.float32,
    ).astype(jnp.bfloat16)
    shaped = [
        member.reshape(part_rows, graph_count * half_heads, HD)
        for member in (query, keys_in, values_in, attn_grad)
    ]
    packed = jnp.stack(shaped, axis=2).reshape(part_rows, graph_count * half_heads, 4 * HD)
    arrived = lax.all_to_all(packed, "head", split_axis=1, concat_axis=0, tiled=True).reshape(
        graph_nodes, 4, HD
    )
    position = lax.axis_index("head")
    graph = position // half_heads
    order = lax.dynamic_index_in_dim(perm, graph, 0, keepdims=False)
    inverse = (
        jnp.zeros((graph_nodes,), jnp.int32).at[order].set(jnp.arange(graph_nodes, dtype=jnp.int32))
    )
    by_node = jnp.take(arrived, inverse, axis=0).reshape(block_count, BS, 4, HD)
    query_blk = by_node[:, :, 0]
    keyval = by_node[:, :, 1:3].reshape(block_count, BS, 2 * HD)
    grad_blk = by_node[:, :, 3]
    block_row = lax.dynamic_index_in_dim(blocks, graph, 0, keepdims=False)
    count_row = lax.dynamic_index_in_dim(counts, graph, 0, keepdims=False)
    live = jnp.arange(KB, dtype=jnp.int32)[None, :] < count_row[:, None]

    def one_group(carry, first):
        queries = lax.dynamic_slice_in_dim(query_blk, first, group_size, 0)
        grads = lax.dynamic_slice_in_dim(grad_blk, first, group_size, 0)
        listed = lax.dynamic_slice_in_dim(block_row, first, group_size, 0)
        active = lax.dynamic_slice_in_dim(live, first, group_size, 0)
        fetched = jnp.take(keyval, listed, axis=0)
        fetched_keys = fetched[..., :HD]
        fetched_values = fetched[..., HD:]
        score = (
            jnp.einsum("qad,qjcd->qajc", queries, fetched_keys, preferred_element_type=jnp.float32)
            * scale
        )
        score = jnp.where(active[:, None, :, None], score, -jnp.inf)
        top = jnp.max(score, axis=(2, 3), keepdims=True)
        expo = jnp.exp(score - top)
        prob = expo / jnp.sum(expo, axis=(2, 3), keepdims=True)
        prob_b = prob.astype(jnp.bfloat16)
        attn = jnp.einsum(
            "qajc,qjcd->qad", prob_b, fetched_values, preferred_element_type=jnp.float32
        )
        delta = jnp.sum(grads.astype(jnp.float32) * attn, axis=-1)
        dprob = jnp.einsum(
            "qad,qjcd->qajc", grads, fetched_values, preferred_element_type=jnp.float32
        )
        dscore = (prob * (dprob - delta[:, :, None, None])).astype(jnp.bfloat16)
        query_grad = (
            jnp.einsum("qajc,qjcd->qad", dscore, fetched_keys, preferred_element_type=jnp.float32)
            * scale
        )
        key_terms = (
            jnp.einsum("qajc,qad->qjcd", dscore, queries, preferred_element_type=jnp.float32)
            * scale
        )
        value_terms = jnp.einsum(
            "qajc,qad->qjcd", prob_b, grads, preferred_element_type=jnp.float32
        )
        update = jnp.concatenate((key_terms, value_terms), axis=-1)
        return (carry.at[listed].add(update), query_grad)

    firsts = jnp.arange(block_count // group_size, dtype=jnp.int32) * group_size
    keyval_grad, query_grads = lax.scan(
        one_group, jnp.zeros((block_count, BS, 2 * HD), jnp.float32), firsts
    )
    all_grads = jnp.concatenate(
        (query_grads.reshape(graph_nodes, HD), keyval_grad.reshape(graph_nodes, 2 * HD)), axis=1
    )
    all_grads = all_grads.astype(jnp.bfloat16)
    by_part = jnp.take(all_grads, order, axis=0).reshape(graph_nodes, 1, 3 * HD)
    returned = lax.all_to_all(by_part, "head", split_axis=0, concat_axis=1, tiled=True).reshape(
        local_rows, half_heads, 3, HD
    )
    full_width = w_query.shape[0]

    def term_for(weight, member):
        shaped_weight = weight.reshape(full_width, half_heads, HD)
        piece = returned[:, :, member]
        return jnp.einsum("rhd,ehd->re", piece, shaped_weight, preferred_element_type=jnp.float32)

    total = lax.psum_scatter(term_for(w_query, 0), "tensor", scatter_dimension=0, tiled=True)
    total = total + lax.psum_scatter(term_for(w_key, 1), "tensor", scatter_dimension=0, tiled=True)
    total = total + lax.psum_scatter(
        term_for(w_value, 2), "tensor", scatter_dimension=0, tiled=True
    )
    return total.astype(jnp.bfloat16)


def solution(mesh):
    return jax.shard_map(
        on_device,
        mesh=mesh,
        in_specs=(
            P(("groups", "head"), "tensor"),
            P(("groups", "head"), "tensor"),
            P(("groups", "head"), "tensor"),
            P(("groups", "head"), "tensor"),
            P("tensor", None),
            P(None, "tensor"),
            P(None, "tensor"),
            P(None, "tensor"),
            P("groups", None),
            P("groups", None, None),
            P("groups", None),
        ),
        out_specs=P(("groups", "head", "tensor"), None),
        check_vma=False,
    )
```

profile of v0, /device:TPU:13, one launch (start us, length us, event | category | flops | bytes accessed | tf_op | source)
XLA Modules:
  0.0 486.9 jit_solution(12786083107851520610)
XLA Ops:
  10.0 9.8 %all-gather.2.cloned.1.call-done = bf16[512,1024]{1,0:T(8,128)(2,1)} async-done(((bf16[512,512]{1,0:T(8,128)(2,1)}), bf16[512,1024]{1,0:T(8,128)(2,1)}) %all-gather.2.cloned.1.call-update) | async-done | bytes 1048592 | tf_op jit(solution)/shard_map/all_gather | solution.py:22
  23.6 5.6 %all-to-all-start = ((bf16[512,8,256]{0,2,1:T(8,128)(2,1)}), bf16[512,8,256]{0,2,1:T(8,128)(2,1)S(1)}, u32[]{:S(2)}, u32[]{:S(2)}) async-start(bf16[512,8,256]{0,2,1:T(8,128)(2,1)} %bitcast.136), calls=%async_computation | async-start | bytes 4194304 | tf_op jit(solution)/shard_map/all_to_all | solution.py:32
  29.3 15.7 %scatter_custom_fusion.1 = s32[4096]{0:T(1024)S(1)} fusion(s32[4096]{0:T(1024)S(1)} %bitcast.150, s32[4096]{0:T(1024)S(1)} %iota.11, s32[]{:T(128)} %constant.74.clone.1), kind=kCustom, calls=%fused_computation.62 | custom fusion | bytes 16388 | tf_op jit(solution)/shard_map/scatter | solution.py:39
  45.2 29.7 %all-to-all-done = bf16[512,8,256]{0,2,1:T(8,128)(2,1)S(1)} async-done(((bf16[512,8,256]{0,2,1:T(8,128)(2,1)}), bf16[512,8,256]{0,2,1:T(8,128)(2,1)S(1)}, u32[]{:S(2)}, u32[]{:S(2)}) %all-to-all-start) | async-done | bytes 2097184 | tf_op jit(solution)/shard_map/all_to_all | solution.py:32
  79.1 3.3 reshape.170
  82.3 30.7 %gather_fusion.1 = bf16[4096,4,64]{2,1,0:T(4,128)(2,1)} fusion(bf16[4096,4,64]{2,1,0:T(4,128)(2,1)} %reshape.170, s32[4096]{0:T(1024)S(1)} %fusion.24), kind=kCustom, calls=%fused_computation.1 | custom fusion | bytes 4210688 | tf_op jit(solution)/shard_map/jit(_take)/gather | solution.py:41
  113.0 4.8 copy.145
  121.7 248.4 %while.12 = (s32[]{:T(128)}, f32[32,128,128]{2,1,0:T(8,128)}, bf16[8,4,128,64]{2,3,1,0:T(8,128)(2,1)}, s32[8]{0:T(128)S(1)}, s32[32,12]{1,0:T(8,128)S(1)}, /*ind...) while((s32[]{:T(128)}, f32[32,128,128]{2,1,0:T(8,128)}, ...), condition=%wide.region_6.7_spmd, body=%wide.region_1.0_spmd.sunk | while | flops 625737472 | bytes 73627488 | solution.py:89
  140.9 9.2 %scatter_fusion = f32[32,128,128]{2,1,0:T(8,128)} fusion(f32[32,128,128]{2,1,0:T(8,128)} %get-tuple-element.203, s32[48]{0:T(128)S(1)} %reshape.184, f32[48,128,128]{2,1,0:T(8,128)S(1)} %copy.192), kind=kCustom, calls=%fused_computation.3.clone.1 | custom fusion | flops 786432 | bytes 9437376 | tf_op jit(solution)/shard_map/while/body/eval_jaxpr/scatter-add | solution.py:86
  172.1 9.0 %scatter_fusion = f32[32,128,128]{2,1,0:T(8,128)} fusion(f32[32,128,128]{2,1,0:T(8,128)} %get-tuple-element.203, s32[48]{0:T(128)S(1)} %reshape.184, f32[48,128,128]{2,1,0:T(8,128)S(1)} %copy.192), kind=kCustom, calls=%fused_computation.3.clone.1 | custom fusion | flops 786432 | bytes 9437376 | tf_op jit(solution)/shard_map/while/body/eval_jaxpr/scatter-add | solution.py:86
  203.2 9.0 %scatter_fusion = f32[32,128,128]{2,1,0:T(8,128)} fusion(f32[32,128,128]{2,1,0:T(8,128)} %get-tuple-element.203, s32[48]{0:T(128)S(1)} %reshape.184, f32[48,128,128]{2,1,0:T(8,128)S(1)} %copy.192), kind=kCustom, calls=%fused_computation.3.clone.1 | custom fusion | flops 786432 | bytes 9437376 | tf_op jit(solution)/shard_map/while/body/eval_jaxpr/scatter-add | solution.py:86
  234.2 9.1 %scatter_fusion = f32[32,128,128]{2,1,0:T(8,128)} fusion(f32[32,128,128]{2,1,0:T(8,128)} %get-tuple-element.203, s32[48]{0:T(128)S(1)} %reshape.184, f32[48,128,128]{2,1,0:T(8,128)S(1)} %copy.192), kind=kCustom, calls=%fused_computation.3.clone.1 | custom fusion | flops 786432 | bytes 9437376 | tf_op jit(solution)/shard_map/while/body/eval_jaxpr/scatter-add | solution.py:86
  265.3 9.0 %scatter_fusion = f32[32,128,128]{2,1,0:T(8,128)} fusion(f32[32,128,128]{2,1,0:T(8,128)} %get-tuple-element.203, s32[48]{0:T(128)S(1)} %reshape.184, f32[48,128,128]{2,1,0:T(8,128)S(1)} %copy.192), kind=kCustom, calls=%fused_computation.3.clone.1 | custom fusion | flops 786432 | bytes 9437376 | tf_op jit(solution)/shard_map/while/body/eval_jaxpr/scatter-add | solution.py:86
  296.4 9.0 %scatter_fusion = f32[32,128,128]{2,1,0:T(8,128)} fusion(f32[32,128,128]{2,1,0:T(8,128)} %get-tuple-element.203, s32[48]{0:T(128)S(1)} %reshape.184, f32[48,128,128]{2,1,0:T(8,128)S(1)} %copy.192), kind=kCustom, calls=%fused_computation.3.clone.1 | custom fusion | flops 786432 | bytes 9437376 | tf_op jit(solution)/shard_map/while/body/eval_jaxpr/scatter-add | solution.py:86
  327.3 9.1 %scatter_fusion = f32[32,128,128]{2,1,0:T(8,128)} fusion(f32[32,128,128]{2,1,0:T(8,128)} %get-tuple-element.203, s32[48]{0:T(128)S(1)} %reshape.184, f32[48,128,128]{2,1,0:T(8,128)S(1)} %copy.192), kind=kCustom, calls=%fused_computation.3.clone.1 | custom fusion | flops 786432 | bytes 9437376 | tf_op jit(solution)/shard_map/while/body/eval_jaxpr/scatter-add | solution.py:86
  358.4 9.0 %scatter_fusion = f32[32,128,128]{2,1,0:T(8,128)} fusion(f32[32,128,128]{2,1,0:T(8,128)} %get-tuple-element.203, s32[48]{0:T(128)S(1)} %reshape.184, f32[48,128,128]{2,1,0:T(8,128)S(1)} %copy.192), kind=kCustom, calls=%fused_computation.3.clone.1 | custom fusion | flops 786432 | bytes 9437376 | tf_op jit(solution)/shard_map/while/body/eval_jaxpr/scatter-add | solution.py:86
  374.3 16.9 %gather_fusion.2 = bf16[4096,192]{1,0:T(8,128)(2,1)} fusion(bf16[4096,192]{1,0:T(8,128)(2,1)S(1)} %pad_maximum_fusion.2, s32[4096]{0:T(1024)S(1)} %broadcast_clamp_fusion), kind=kCustom, calls=%fused_computation.2 | custom fusion | bytes 3162112 | tf_op jit(solution)/shard_map/jit(_take)/gather | solution.py:96
  393.7 3.1 reduce
  396.8 6.7 %reshape.173 = bf16[8,2,49152]{2,1,0:T(2,128)(2,1)} reshape(bf16[4096,192]{1,0:T(8,128)(2,1)} %reduce) | data formatting | bytes 3145728
  403.5 6.5 %all-to-all-start.1 = ((bf16[8,2,49152]{2,1,0:T(2,128)(2,1)}), bf16[8,2,49152]{2,1,0:T(2,128)(2,1)S(1)}, u32[]{:S(2)}, u32[]{:S(2)}) async-start(bf16[8,2,49152]{2,1,0:T(2,128)(2,1)} %reshape.173), calls=%async_computation.1 | async-start | bytes 3145728 | tf_op jit(solution)/shard_map/all_to_all | solution.py:97
  415.0 29.5 %all-to-all-done.1 = bf16[8,2,49152]{2,1,0:T(2,128)(2,1)S(1)} async-done(((bf16[8,2,49152]{2,1,0:T(2,128)(2,1)}), bf16[8,2,49152]{2,1,0:T(2,128)(2,1)S(1)}, u32[]{:S(2)}, u32[]{:S(2)}) %all-to-all-start.1) | async-done | bytes 1572896 | tf_op jit(solution)/shard_map/all_to_all | solution.py:97
  444.5 4.9 %reshape.174 = bf16[4096,1,192]{2,1,0:T(2,128)(2,1)} reshape(bf16[8,2,49152]{2,1,0:T(2,128)(2,1)S(1)} %all-to-all-done.1) | data formatting | bytes 3145728
  449.3 9.9 %copy.127 = bf16[4096,1,192]{0,2,1:T(8,128)(2,1)S(1)} copy(bf16[4096,1,192]{2,1,0:T(2,128)(2,1)} %reshape.174) | data formatting | bytes 3145728 | tf_op jit(solution)/shard_map/all_to_all | solution.py:97
  465.7 12.3 %reduce-scatter.2.cloned.1.call-done = f32[256,1024]{1,0:T(8,128)} async-done(((f32[512,1024]{1,0:T(8,128)}), f32[256,1024]{1,0:T(8,128)}) %reduce-scatter.2.cloned.1.call-update) | async-done | bytes 1048592 | tf_op jit(solution)/shard_map/reduce_scatter | solution.py:107
  (248 shorter events, 196.2 us)
Async XLA Ops:
  6.5 13.2 %copy-start = (bf16[512,1024]{1,0:T(8,128)(2,1)S(1)}, bf16[512,1024]{1,0:T(8,128)(2,1)}, u32[]{:S(2)}) copy-start(bf16[512,1024]{1,0:T(8,128)(2,1)} %param.17) | copy-start | bytes 3145732
  6.5 3.2 copy-start.11
  6.5 13.2 %all-gather.2.cloned.1.call-start = ((), (), s32[]{:S(2)}) async-start(), calls=%async_computation.3 | async-start | bytes 1572864 | tf_op jit(solution)/shard_map/all_gather | solution.py:22
  23.6 5.6 %copy-start.13 = (s32[1,32,12]{1,0,2:T(1,128)S(1)}, s32[1,32,12]{1,0,2:T(1,128)}, u32[]{:S(2)}) copy-start(s32[1,32,12]{1,0,2:T(1,128)} %param.22) | copy-start | bytes 4612
  23.6 5.7 %copy-start.12 = (s32[1,4096]{1,0:T(1,128)S(1)}, s32[1,4096]{1,0:T(1,128)}, u32[]{:S(2)}) copy-start(s32[1,4096]{1,0:T(1,128)} %param.21) | copy-start | bytes 49156
  23.6 21.5 %copy-start.14 = (s32[1,32]{1,0:T(1,128)S(1)}, s32[1,32]{1,0:T(1,128)}, u32[]{:S(2)}) copy-start(s32[1,32]{1,0:T(1,128)} %param.23) | copy-start | bytes 388
  23.6 51.3 %all-to-all-start = ((bf16[512,8,256]{0,2,1:T(8,128)(2,1)}), bf16[512,8,256]{0,2,1:T(8,128)(2,1)S(1)}, u32[]{:S(2)}, u32[]{:S(2)}) async-start(bf16[512,8,256]{0,2,1:T(8,128)(2,1)} %bitcast.136), calls=%async_computation | async-start | bytes 4194304 | tf_op jit(solution)/shard_map/all_to_all | solution.py:32
  126.4 4.3 copy-start.2
  150.1 2.8 copy-start.4
  157.6 4.3 copy-start.2
  181.2 2.8 copy-start.4
  188.7 4.3 copy-start.2
  219.7 4.3 copy-start.2
  243.3 2.8 copy-start.4
  250.8 4.3 copy-start.2
  274.3 2.8 copy-start.4
  281.8 4.3 copy-start.2
  312.9 4.2 copy-start.2
  343.9 4.2 copy-start.2
  367.3 2.8 copy-start.4
  403.5 6.5 %copy-start.6 = (bf16[1024,512]{1,0:T(8,128)(2,1)S(1)}, bf16[1024,512]{1,0:T(8,128)(2,1)}, u32[]{:S(2)}) copy-start(bf16[1024,512]{1,0:T(8,128)(2,1)} %param.18) | copy-start | bytes 3145732
  403.5 41.0 %all-to-all-start.1 = ((bf16[8,2,49152]{2,1,0:T(2,128)(2,1)}), bf16[8,2,49152]{2,1,0:T(2,128)(2,1)S(1)}, u32[]{:S(2)}, u32[]{:S(2)}) async-start(bf16[8,2,49152]{2,1,0:T(2,128)(2,1)} %reshape.173), calls=%async_computation.1 | async-start | bytes 3145728 | tf_op jit(solution)/shard_map/all_to_all | solution.py:97
  410.0 68.0 %reduce-scatter.2.cloned.1.call-start = ((), (), s32[]{:S(2)}) async-start(), calls=%async_computation.4 | async-start | bytes 3145728 | tf_op jit(solution)/shard_map/reduce_scatter | solution.py:107
  463.6 16.5 %copy-start.1 = (bf16[512,1024]{1,0:T(8,128)(2,1)S(1)}, bf16[512,1024]{1,0:T(8,128)(2,1)}, u32[]{:S(2)}) copy-start(bf16[512,1024]{1,0:T(8,128)(2,1)} %param.17) | copy-start | bytes 3145732
  (16 other events, 37.5 us)
Sparse Core Ops, SparseCore 0:
  8.9 10.8 all-gather.1
  465.8 12.1 reduce-scatter.1
where the time goes:
time: 491 us; the launch traced here: 487 us
  local copies, waits for them, and re-layouts  166 us (34%)
  other arithmetic  107 us (22%)
  matrix products  90.5 us (18%)
  waiting for transfers between devices  82 us (17%)
  loops' own time  15.5 us (3%)
  between operations  13.6 us (3%)
  starting transfers between devices  12.1 us (2%)
    scatter-add x8, other arithmetic, one_group(): return (carry.at[listed].add(update), query_grad)  72.3 us
    gather x2, local copies, waits for them, and re-layouts, on_device(): by_node = jnp.take(arrived, inverse, axis=0).reshape(block_count, BS, 4, HD)  35.4 us
    all_to_all x1, waiting for transfers between devices, on_device(): lax.all_to_all(packed, 'head', split_axis=1, concat_axis=0, tiled=True)  29.7 us
    all_to_all x1, waiting for transfers between devices, on_device(): lax.all_to_all(by_part, 'head', split_axis=0, concat_axis=1, tiled=True)  29.5 us
    unnamed x34, local copies, waits for them, and re-layouts  23.4 us
    dot_general x8, matrix products, one_group(): jnp.einsum('qajc,qjcd->qad', dscore, fetched_keys, preferred_element_type...  22.4 us
    dot_general x8, matrix products, one_group(): jnp.einsum('qad,qjcd->qajc', grads, fetched_values, preferred_element_typ...  22 us
    concatenate x8, local copies, waits for them, and re-layouts, one_group(): update = jnp.concatenate((key_terms, value_terms), axis=-1)  19 us
  transfers between devices with their start and end apart: 4, of which 4 were waited for; matrix products, arithmetic and copies ran while one was open for 5% of the time, Pallas kernels for 0%

commit v1 on v0

v1 whole, which is shorter than its diff:
```python
import functools

import jax
import jax.numpy as jnp
from jax import lax
from jax.experimental import pallas as pl
from jax.experimental.pallas import tpu as pltpu
from jax.sharding import PartitionSpec as P

HD = 64
BS = 128
KB = 12
NT = (((1,), (1,)), ((), ()))
STEP = 4


def dot(a, b):
    return jnp.dot(a, b, preferred_element_type=jnp.float32)


def attend(block_ref, count_ref, row_ref, col_ref, x_ref, out_ref, kv_s, kt_s, qg_s, dkv_s, g_s, s_s, d_s):
    nodes = x_ref.shape[0]
    block_count = nodes // BS
    parts, out_rows, _ = out_ref.shape
    half = out_rows // 3
    scale = HD ** (-0.5)
    low = lax.broadcasted_iota(jnp.int32, (BS, 2 * HD), 1) < HD

    @pl.loop(0, block_count // 2)
    def _(i):
        ids = lax.broadcasted_iota(jnp.int32, (2 * BS, nodes), 0) + i * (2 * BS)
        hot = jnp.where(ids == row_ref[...], 1.0, 0.0).astype(jnp.bfloat16)
        got = dot(hot, x_ref[...])
        for u in range(2):
            b = i * 2 + u
            qg = got[u * BS:(u + 1) * BS, :2 * HD]
            kv = got[u * BS:(u + 1) * BS, 2 * HD:]
            qg_s[b, :BS] = jnp.where(low, qg * scale, 0.0).astype(jnp.bfloat16)
            qg_s[b, BS:] = jnp.where(low, 0.0, qg).astype(jnp.bfloat16)
            kv_s[b] = kv.astype(jnp.bfloat16)
            kt = (kv.T[:HD] * scale).astype(jnp.bfloat16)
            kt_s[b, :HD] = kt
            kt_s[b, HD:] = kt
            dkv_s[b] = jnp.zeros((BS, 2 * HD), jnp.float32)

    def one_block(b, count, slots):
        qg = qg_s[b]
        listed = [block_ref[b, j] for j in range(slots)]
        top = None
        for j in range(slots):
            sd = lax.dot_general(kv_s[listed[j]], qg, NT, preferred_element_type=jnp.float32)
            s = sd[:, :BS]
            if j > slots - STEP:
                s = jnp.where(j < count, s, -jnp.inf)
            s_s[j] = s
            d_s[j] = sd[:, BS:]
            top = s if top is None else jnp.maximum(top, s)
        top = jnp.max(top, axis=0, keepdims=True)
        norm = weighted = None
        for j in range(slots):
            e = jnp.exp(s_s[j] - top)
            s_s[j] = e
            ed = e * d_s[j]
            norm = e if norm is None else norm + e
            weighted = ed if weighted is None else weighted + ed
        inv = 1.0 / jnp.sum(norm, axis=0, keepdims=True)
        delta = jnp.sum(weighted, axis=0, keepdims=True) * inv
        dqt = None
        for j in range(0, slots, 2):
            ds_pair = []
            updates = []
            for k in (j, j + 1):
                p = s_s[k] * inv
                ds = (p * (d_s[k] - delta)).astype(jnp.bfloat16)
                ds_pair.append(ds)
                updates.append(dot(jnp.concatenate((ds, p.astype(jnp.bfloat16)), axis=1), qg))
            kt = jnp.concatenate((kt_s[listed[j]], kt_s[listed[j + 1]]), axis=1)
            term = dot(kt, jnp.concatenate(ds_pair, axis=0))
            dqt = term if dqt is None else dqt + term
            for k in (0, 1):
                dkv_s[listed[j + k]] += updates[k]
        g_s[pl.ds(pl.multiple_of(b * BS, BS), BS), 2 * HD:] = dqt.T.astype(jnp.bfloat16)

    @pl.loop(0, block_count)
    def _(b):
        count = count_ref[b]
        for slots in range(STEP, KB + 1, STEP):
            @pl.when((count > slots - STEP) & (count <= slots))
            def _():
                one_block(b, count, slots)

    @pl.loop(0, block_count)
    def _(b):
        g_s[pl.ds(pl.multiple_of(b * BS, BS), BS), :2 * HD] = dkv_s[b].astype(jnp.bfloat16)

    @pl.loop(0, parts)
    def _(i):
        halves = []
        for u in range(2):
            start = pl.multiple_of((i * 2 + u) * half, half)
            ids = lax.broadcasted_iota(jnp.int32, (half, nodes), 1)
            hot = jnp.where(ids == col_ref[pl.ds(start, half), :], 1.0, 0.0).astype(jnp.bfloat16)
            got = dot(hot, g_s[...])
            out_ref[i, u * half:(u + 1) * half] = got[:, :2 * HD].astype(jnp.bfloat16)
            halves.append(got[:, 2 * HD:])
        keep = lax.broadcasted_iota(jnp.int32, (half, 2 * HD), 1) < HD
        out_ref[i, 2 * half:] = jnp.where(keep, halves[0], halves[1]).astype(jnp.bfloat16)


def attention(x, order, block_row, count_row, parts):
    nodes = x.shape[0]
    block_count = nodes // BS
    vmem = pl.BlockSpec(memory_space=pltpu.VMEM)
    smem = pl.BlockSpec(memory_space=pltpu.SMEM)
    return pl.pallas_call(
        attend,
        out_shape=jax.ShapeDtypeStruct((parts, nodes // parts * 3 // 2, 2 * HD), jnp.bfloat16),
        in_specs=[smem, smem, vmem, vmem, vmem],
        out_specs=vmem,
        scratch_shapes=[
            pltpu.VMEM((block_count, BS, 2 * HD), jnp.bfloat16),
            pltpu.VMEM((block_count, 2 * HD, BS), jnp.bfloat16),
            pltpu.VMEM((block_count, 2 * BS, 2 * HD), jnp.bfloat16),
            pltpu.VMEM((block_count, BS, 2 * HD), jnp.float32),
            pltpu.VMEM((nodes, 4 * HD), jnp.bfloat16),
            pltpu.VMEM((KB, BS, BS), jnp.float32),
            pltpu.VMEM((KB, BS, BS), jnp.float32),
        ],
        compiler_params=pltpu.CompilerParams(vmem_limit_bytes=48 << 20),
        name="attend",
    )(block_row, count_row, order.reshape(1, nodes), order.reshape(nodes, 1), x)


def project(side_ref, rec_ref, wq_ref, wk_ref, wv_ref, keep_ref, send_ref, aq, ak, av):
    heads, out_rows, _ = rec_ref.shape
    half = out_rows // 3
    for h in range(heads):
        cols = slice(h * HD, (h + 1) * HD)
        aq[:half, cols] = rec_ref[h, 2 * half:, :HD]
        aq[half:, cols] = rec_ref[h, 2 * half:, HD:]
        ak[:, cols] = rec_ref[h, :2 * half, :HD]
        av[:, cols] = rec_ref[h, :2 * half, HD:]
    side = side_ref[0]

    def rows_at(part):
        rows = pl.ds(pl.multiple_of(part * half, half), half)
        total = lax.dot_general(aq[rows], wq_ref[...], NT, preferred_element_type=jnp.float32)
        total += lax.dot_general(ak[rows], wk_ref[...], NT, preferred_element_type=jnp.float32)
        total += lax.dot_general(av[rows], wv_ref[...], NT, preferred_element_type=jnp.float32)
        return total

    send_ref[...] = rows_at(1 - side).astype(jnp.bfloat16)
    keep_ref[...] = rows_at(side)


def projection(side, received, w_query, w_key, w_value, graphs):
    total_heads, out_rows, _ = received.shape
    heads = total_heads // graphs
    half = out_rows // 3
    full, width = w_query.shape
    weight = pl.BlockSpec((full, width), lambda g: (0, 0))
    result = pl.BlockSpec((None, half, full), lambda g: (g, 0, 0))
    return pl.pallas_call(
        project,
        grid=(graphs,),
        out_shape=(
            jax.ShapeDtypeStruct((graphs, half, full), jnp.float32),
            jax.ShapeDtypeStruct((graphs, half, full), jnp.bfloat16),
        ),
        in_specs=[
            pl.BlockSpec(memory_space=pltpu.SMEM),
            pl.BlockSpec((heads, out_rows, 2 * HD), lambda g: (g, 0, 0)),
            weight, weight, weight,
        ],
        out_specs=(result, result),
        scratch_shapes=[pltpu.VMEM((2 * half, width), jnp.bfloat16)] * 3,
        compiler_params=pltpu.CompilerParams(vmem_limit_bytes=48 << 20),
        name="project",
    )(side, received, w_query, w_key, w_value)


def on_device(
    query, keys_in, values_in, grad_out, w_out, w_query, w_key, w_value, perm, blocks, counts
):
    local_rows, half_width = query.shape
    graphs, nodes = perm.shape
    half_heads = half_width // HD
    part_rows = local_rows // graphs
    parts = nodes // part_rows
    attn_grad = lax.dot_general(
        lax.all_gather(grad_out, "tensor", axis=1, tiled=True),
        w_out,
        NT,
        preferred_element_type=jnp.float32,
    ).astype(jnp.bfloat16)
    packed = jnp.concatenate(
        [
            member.reshape(part_rows, graphs * half_heads, HD).transpose(1, 0, 2)
            for member in (query, attn_grad, keys_in, values_in)
        ],
        axis=2,
    )
    arrived = lax.all_to_all(packed, "head", split_axis=0, concat_axis=0, tiled=True)
    graph = lax.axis_index("head") // half_heads
    order = lax.dynamic_index_in_dim(perm, graph, 0, keepdims=False)
    block_row = lax.dynamic_index_in_dim(blocks, graph, 0, keepdims=False)
    count_row = lax.dynamic_index_in_dim(counts, graph, 0, keepdims=False)
    by_part = attention(arrived.reshape(nodes, 4 * HD), order, block_row, count_row, parts)
    returned = lax.all_to_all(by_part, "head", split_axis=0, concat_axis=0, tiled=True)
    side = lax.axis_index("tensor").astype(jnp.int32).reshape(1)
    keep, send = projection(side, returned, w_query, w_key, w_value, graphs)
    got = lax.ppermute(send, "tensor", [(0, 1), (1, 0)])
    total = (keep + got.astype(jnp.float32)).astype(jnp.bfloat16)
    return total.transpose(1, 0, 2).reshape(local_rows // 2, -1)


def solution(mesh):
    return jax.shard_map(
        on_device,
        mesh=mesh,
        in_specs=(
            P(("groups", "head"), "tensor"),
            P(("groups", "head"), "tensor"),
            P(("groups", "head"), "tensor"),
            P(("groups", "head"), "tensor"),
            P("tensor", None),
            P(None, "tensor"),
            P(None, "tensor"),
            P(None, "tensor"),
            P("groups", None),
            P("groups", None, None),
            P("groups", None),
        ),
        out_specs=P(("groups", "head", "tensor"), None),
        check_vma=False,
    )
```

time: 491 us -> 193 us (0.39)
  the two profiles are of different devices: /device:TPU:13 before, /device:TPU:0 now
where the time goes in v1:
time: 193 us; the launch traced here: 192 us
  waiting for transfers between devices  97.9 us (51%)
  Pallas kernels  54.3 us (28%)
  between operations  13.5 us (7%)
  local copies, waits for them, and re-layouts  11.4 us (6%)
  starting transfers between devices  10.4 us (5%)
  other arithmetic  2.48 us (1%)
  matrix products  1.96 us (1%)
    pallas_call x1, Pallas kernels, attention(): pl.pallas_call(attend, out_shape=jax.ShapeDtypeStruct((parts, nodes // pa...  50.8 us
    all_to_all x1, waiting for transfers between devices, on_device(): lax.all_to_all(packed, 'head', split_axis=0, concat_axis=0, tiled=True)  48 us
    all_to_all x1, waiting for transfers between devices, on_device(): lax.all_to_all(by_part, 'head', split_axis=0, concat_axis=0, tiled=True)  36.6 us
    all_gather x1, waiting for transfers between devices, on_device(): lax.all_gather(grad_out, 'tensor', axis=1, tiled=True)  10.7 us
    unnamed x24, local copies, waits for them, and re-layouts  6.81 us
    all_to_all x1, starting transfers between devices, on_device(): lax.all_to_all(packed, 'head', split_axis=0, concat_axis=0, tiled=True)  5.92 us
    all_to_all x1, starting transfers between devices, on_device(): lax.all_to_all(by_part, 'head', split_axis=0, concat_axis=0, tiled=True)  4.44 us
    all_to_all x1, local copies, waits for them, and re-layouts, on_device(): lax.all_to_all(packed, 'head', split_axis=0, concat_axis=0, tiled=True)  3.91 us
  transfers between devices with their start and end apart: 4, of which 4 were waited for; matrix products, arithmetic and copies ran while one was open for 2% of the time, Pallas kernels for 0%

profile of v1, /device:TPU:0, one launch (start us, length us, event | category | flops | bytes accessed | tf_op | source)
XLA Modules:
  0.0 191.9 jit_solution(11305714056421297027)
XLA Ops:
  6.5 0.7 all-gather.2.cloned.1.call-update
  7.3 1.3 copy.20
  8.5 1.3 copy.18
  9.8 0.0 copy-done.8
  9.8 0.2 copy.19
  10.0 10.7 %all-gather.2.cloned.1.call-done = bf16[512,1024]{1,0:T(8,128)(2,1)} async-done(((bf16[512,512]{1,0:T(8,128)(2,1)}), bf16[512,1024]{1,0:T(8,128)(2,1)}) %all-gather.2.cloned.1.call-update) | async-done | bytes 1048592 | tf_op jit(solution)/shard_map/all_gather | solution.py:191
  20.7 2.0 %convolution_convert_fusion = bf16[512,512]{0,1:T(8,128)(2,1)S(1)} fusion(bf16[512,1024]{1,0:T(8,128)(2,1)} %all-gather.2.cloned.1.call-done, bf16[512,1024]{1,0:T(8,128)(2,1)S(1)} %copy-done), kind=kOutput, calls=%fused_computation.1 | convolution fusion | flops 537133056 | bytes 2621440 | tf_op jit(solution)/shard_map/dot_general | solution.py:190
  22.6 1.5 pad_maximum_fusion
  24.2 5.9 %all-to-all-start = ((bf16[8,512,256]{1,2,0:T(8,128)(2,1)}), bf16[8,512,256]{1,2,0:T(8,128)(2,1)}, u32[]{:S(2)}, u32[]{:S(2)}) async-start(bf16[8,512,256]{1,2,0:T(8,128)(2,1)} %pad_maximum_fusion), calls=%async_computation | async-start | bytes 4194304 | tf_op jit(solution)/shard_map/all_to_all | solution.py:203
  30.1 0.6 copy.22.col_ref
  30.8 0.0 copy-done.9
  30.8 0.1 copy.17
  30.9 48.0 %all-to-all-done = bf16[8,512,256]{1,2,0:T(8,128)(2,1)} async-done(((bf16[8,512,256]{1,2,0:T(8,128)(2,1)}), bf16[8,512,256]{1,2,0:T(8,128)(2,1)}, u32[]{:S(2)}, u32[]{:S(2)}) %all-to-all-start) | async-done | bytes 2097184 | tf_op jit(solution)/shard_map/all_to_all | solution.py:203
  78.9 3.9 %copy.21 = bf16[8,512,256]{2,1,0:T(8,128)(2,1)} copy(bf16[8,512,256]{1,2,0:T(8,128)(2,1)} %all-to-all-done) | data formatting | bytes 4194304 | tf_op jit(solution)/shard_map/all_to_all | solution.py:203
  82.8 1.6 copy-done.1
  84.4 50.8 %attend.1 = bf16[8,768,128]{2,1,0:T(8,128)(2,1)S(1)} custom-call(s32[32,12]{1,0:T(8,128)S(1)} %bitcast.23, s32[32]{0:T(128)S(1)} %bitcast.24, s32[1,4096]{1,0:T(1,128)S(1)} %copy-done.6, s32[4096,1]{1,0:T(8,128)S(1)} %copy.22.col_ref, bf16[4096,256]{1,0:T(8,128)(2,1)S(1)} %bitcast.21), custom_call_target="tpu_custom_call" | custom-call | tf_op jit(solution)/shard_map/attend/pallas_call | solution.py:115
  135.2 1.1 copy-done.2
  136.3 4.4 %all-to-all-start.1 = ((bf16[8,768,128]{2,1,0:T(8,128)(2,1)}), bf16[8,768,128]{2,1,0:T(8,128)(2,1)}, u32[]{:S(2)}, u32[]{:S(2)}) async-start(bf16[8,768,128]{2,1,0:T(8,128)(2,1)} %copy-done.2), calls=%async_computation.1 | async-start | bytes 3145728 | tf_op jit(solution)/shard_map/all_to_all | solution.py:209
  140.8 36.6 %all-to-all-done.1.rec_ref = bf16[8,768,128]{2,1,0:T(8,128)(2,1)} async-done(((bf16[8,768,128]{2,1,0:T(8,128)(2,1)}), bf16[8,768,128]{2,1,0:T(8,128)(2,1)}, u32[]{:S(2)}, u32[]{:S(2)}) %all-to-all-start.1) | async-done | bytes 1572896 | tf_op jit(solution)/shard_map/all_to_all | solution.py:209
  177.4 1.2 copy-done.5
  178.6 3.5 %project.1 = (f32[1,256,1024]{2,1,0:T(8,128)S(1)}, bf16[1,256,1024]{2,1,0:T(8,128)(2,1)S(1)}) custom-call(s32[1]{0:T(128)} %bitcast.side_ref, bf16[8,768,128]{2,1,0:T(8,128)(2,1)} %all-to-all-done.1.rec_ref, bf16[1024,512]{1,0:T(8,128)(2,1)S(1)} %copy-done.3, bf16[1024,512]{1,0:T(8,128)(2,1)S(1)} %copy-done.4, bf16[1024,512]{1,0:T(8,128)(2,1)S(1)} %copy-done.5), custom_call_target="tpu_custom_call" | custom-call | tf_op jit(solution)/shard_map/project/pallas_call | solution.py:163
  182.2 0.1 collective-permute-start
  182.3 1.9 collective-permute-done
  184.2 0.9 fusion
  (16 shorter events, 0.0 us)
Async XLA Ops:
  6.5 14.1 %copy-start = (bf16[512,1024]{1,0:T(8,128)(2,1)S(1)}, bf16[512,1024]{1,0:T(8,128)(2,1)}, u32[]{:S(2)}) copy-start(bf16[512,1024]{1,0:T(8,128)(2,1)} %param.15) | copy-start | bytes 3145732
  6.5 3.2 %copy-start.8 = (bf16[512,512]{1,0:T(8,128)(2,1)S(1)}, bf16[512,512]{1,0:T(8,128)(2,1)}, u32[]{:S(2)}) copy-start(bf16[512,512]{1,0:T(8,128)(2,1)} %param.12) | copy-start | bytes 1572868
  6.5 14.1 %all-gather.2.cloned.1.call-start = ((), (), s32[]{:S(2)}) async-start(), calls=%async_computation.2 | async-start | bytes 1572864 | tf_op jit(solution)/shard_map/all_gather | solution.py:191
  24.2 5.9 %copy-start.6 = (s32[1,4096]{1,0:T(1,128)S(1)}, s32[1,4096]{1,0:T(1,128)}, u32[]{:S(2)}) copy-start(s32[1,4096]{1,0:T(1,128)} %row_ref) | copy-start | bytes 49156
  24.2 54.7 %all-to-all-start = ((bf16[8,512,256]{1,2,0:T(8,128)(2,1)}), bf16[8,512,256]{1,2,0:T(8,128)(2,1)}, u32[]{:S(2)}, u32[]{:S(2)}) async-start(bf16[8,512,256]{1,2,0:T(8,128)(2,1)} %pad_maximum_fusion), calls=%async_computation | async-start | bytes 4194304 | tf_op jit(solution)/shard_map/all_to_all | solution.py:203
  30.1 0.7 copy-start.9
  30.9 51.9 %copy-start.7 = (s32[1,32]{1,0:T(1,128)S(1)}, s32[1,32]{1,0:T(1,128)}, u32[]{:S(2)}) copy-start(s32[1,32]{1,0:T(1,128)} %param.21) | copy-start | bytes 388
  82.8 1.6 copy-start.1
  135.2 1.1 copy-start.2
  136.3 41.1 %copy-start.3 = (bf16[1024,512]{1,0:T(8,128)(2,1)S(1)}, bf16[1024,512]{1,0:T(8,128)(2,1)}, u32[]{:S(2)}) copy-start(bf16[1024,512]{1,0:T(8,128)(2,1)} %wq_ref.1) | copy-start | bytes 3145732
  136.3 41.1 %copy-start.4 = (bf16[1024,512]{1,0:T(8,128)(2,1)S(1)}, bf16[1024,512]{1,0:T(8,128)(2,1)}, u32[]{:S(2)}) copy-start(bf16[1024,512]{1,0:T(8,128)(2,1)} %wk_ref.1) | copy-start | bytes 3145732
  136.3 41.1 %all-to-all-start.1 = ((bf16[8,768,128]{2,1,0:T(8,128)(2,1)}), bf16[8,768,128]{2,1,0:T(8,128)(2,1)}, u32[]{:S(2)}, u32[]{:S(2)}) async-start(bf16[8,768,128]{2,1,0:T(8,128)(2,1)} %copy-done.2), calls=%async_computation.1 | async-start | bytes 3145728 | tf_op jit(solution)/shard_map/all_to_all | solution.py:209
  177.4 1.2 copy-start.5
  182.2 2.0 %collective-permute-start = (bf16[1,256,1024]{2,1,0:T(8,128)(2,1)S(1)}, bf16[1,256,1024]{2,1,0:T(8,128)(2,1)S(1)}, u32[]{:S(2)}, u32[]{:S(2)}) collective-permute-start(bf16[1,256,1024]{2,1,0:T(8,128)(2,1)S(1)} %get-tuple-element.8), channel_id=1, source_target_pairs={{0,1},{1,0},{2,3},{3,2},{4,5},{5,4},{6,7},{7,6},{8,9},{9,8},{10,11... | collective-permute-start | bytes 1572872 | tf_op jit(solution)/shard_map/ppermute | solution.py:212
Sparse Core Ops, SparseCore 0:
  8.9 11.7 all-gather.1

commit v2 on v1

v2 whole, which is shorter than its diff:
```python
import jax
import jax.numpy as jnp
from jax import lax
from jax.experimental import pallas as pl
from jax.experimental.pallas import tpu as pltpu
from jax.sharding import PartitionSpec as P

HD = 64
BS = 128
KB = 12
NT = (((1,), (1,)), ((), ()))
STEP = 4
TILE = 512
MESH = pl.DeviceIdType.MESH


def dot(a, b):
    return jnp.dot(a, b, preferred_element_type=jnp.float32)


def spread(row_ref, q_ref, k_ref, v_ref, go_ref, w_ref, qg_out, kv_out,
           grad_s, attn_s, kv_pack, qg_pack, kv_in, qg_in, acc_s, pair_sem, send_sem, recv_sem):
    n, part_rows, _ = kv_in.shape
    heads = q_ref.shape[1] // HD
    graphs = n // heads
    nodes = n * part_rows
    me = lax.axis_index("head")
    side = lax.axis_index("tensor")
    width = go_ref.shape[1]
    barrier = pltpu.get_barrier_semaphore()
    pl.semaphore_signal(barrier, inc=1, device_id={"tensor": 1 - side}, device_id_type=MESH)

    @pl.loop(1, n)
    def _(k):
        pl.semaphore_signal(barrier, inc=1, device_id={"head": lax.rem(me + k, n)}, device_id_type=MESH)

    @pl.loop(0, graphs)
    def _(g):
        rows = pl.ds(pl.multiple_of(g * part_rows, part_rows), part_rows)
        for h in range(heads):
            cols = slice(h * HD, (h + 1) * HD)
            kv_pack[g * heads + h, :, :HD] = k_ref[rows, cols]
            kv_pack[g * heads + h, :, HD:] = v_ref[rows, cols]
            qg_pack[g * heads + h, :, :HD] = q_ref[rows, cols]

    pl.semaphore_wait(barrier, n)
    pair = pltpu.make_async_remote_copy(
        src_ref=go_ref, dst_ref=grad_s, send_sem=pair_sem.at[0], recv_sem=pair_sem.at[1],
        device_id={"tensor": 1 - side}, device_id_type=MESH,
    )
    pair.start()

    def copy_to(which, pack, land, peer, slot):
        return pltpu.make_async_remote_copy(
            src_ref=pack.at[peer], dst_ref=land.at[slot],
            send_sem=send_sem.at[which, peer], recv_sem=recv_sem.at[which, slot],
            device_id={"head": peer}, device_id_type=MESH,
        )

    def send_all(which, pack, land):
        @pl.loop(1, n)
        def _(k):
            copy_to(which, pack, land, lax.rem(me + k, n), me).start()

    send_all(0, kv_pack, kv_in)
    near = pl.ds(pl.multiple_of(side * width, width), width)
    far = pl.ds(pl.multiple_of((1 - side) * width, width), width)
    attn_s[...] = lax.dot_general(go_ref[...], w_ref[:, near], NT, preferred_element_type=jnp.float32)
    pair.wait()
    attn_s[...] += lax.dot_general(grad_s[...], w_ref[:, far], NT, preferred_element_type=jnp.float32)

    @pl.loop(0, graphs)
    def _(g):
        rows = pl.ds(pl.multiple_of(g * part_rows, part_rows), part_rows)
        for h in range(heads):
            cols = slice(h * HD, (h + 1) * HD)
            qg_pack[g * heads + h, :, HD:] = attn_s[rows, cols].astype(jnp.bfloat16)

    send_all(1, qg_pack, qg_in)

    def gather(which, pack, land, out):
        def add(chunk, source, first):
            @pl.loop(0, nodes // TILE)
            def _(i):
                rows = pl.ds(pl.multiple_of(i * TILE, TILE), TILE)
                ids = lax.broadcasted_iota(jnp.int32, (TILE, part_rows), 0) + i * TILE
                hot = jnp.where(ids == row_ref[source], 1.0, 0.0).astype(jnp.bfloat16)
                if first:
                    acc_s[rows] = dot(hot, chunk)
                else:
                    acc_s[rows] += dot(hot, chunk)

        add(pack[me], me, True)

        @pl.loop(1, n)
        def _(k):
            source = lax.rem(me + n - k, n)
            copy_to(which, pack, land, source, source).wait_recv()
            add(land[source], source, False)

        out[...] = acc_s[...].astype(jnp.bfloat16)

    gather(0, kv_pack, kv_in, kv_out)
    gather(1, qg_pack, qg_in, qg_out)

    @pl.loop(1, n)
    def _(k):
        peer = lax.rem(me + k, n)
        copy_to(0, kv_pack, kv_in, peer, me).wait_send()
        copy_to(1, qg_pack, qg_in, peer, me).wait_send()


def spreading(order, query, keys_in, values_in, grad_out, w_out, n):
    nodes = order.shape[0]
    part_rows = nodes // n
    vmem = pl.BlockSpec(memory_space=pltpu.VMEM)
    chunks = pltpu.VMEM((n, part_rows, 2 * HD), jnp.bfloat16)
    half = jax.ShapeDtypeStruct((nodes, 2 * HD), jnp.bfloat16)
    return pl.pallas_call(
        spread,
        out_shape=(half, half),
        in_specs=[vmem] * 6,
        out_specs=(vmem, vmem),
        scratch_shapes=[
            pltpu.VMEM(grad_out.shape, jnp.bfloat16),
            pltpu.VMEM(query.shape, jnp.float32),
            chunks, chunks, chunks, chunks,
            pltpu.VMEM((nodes, 2 * HD), jnp.float32),
            pltpu.SemaphoreType.DMA((2,)),
            pltpu.SemaphoreType.DMA((2, n)),
            pltpu.SemaphoreType.DMA((2, n)),
        ],
        compiler_params=pltpu.CompilerParams(
            vmem_limit_bytes=48 << 20, collective_id=0, has_side_effects=True
        ),
        name="spread",
    )(order.reshape(n, 1, part_rows), query, keys_in, values_in, grad_out, w_out)


def attend(block_ref, count_ref, qg_ref, kv_ref, out_ref, kt_s, qg_s, dkv_s, s_s, d_s):
    block_count = kv_ref.shape[0]
    scale = HD ** (-0.5)
    low = lax.broadcasted_iota(jnp.int32, (BS, 2 * HD), 1) < HD

    @pl.loop(0, block_count)
    def _(b):
        qg = qg_ref[b].astype(jnp.float32)
        qg_s[b, :BS] = jnp.where(low, qg * scale, 0.0).astype(jnp.bfloat16)
        qg_s[b, BS:] = jnp.where(low, 0.0, qg).astype(jnp.bfloat16)
        kt = (kv_ref[b].astype(jnp.float32).T[:HD] * scale).astype(jnp.bfloat16)
        kt_s[b, :HD] = kt
        kt_s[b, HD:] = kt
        dkv_s[b] = jnp.zeros((BS, 2 * HD), jnp.float32)

    def one_block(b, count, slots):
        qg = qg_s[b]
        listed = [block_ref[b, j] for j in range(slots)]
        top = None
        for j in range(slots):
            sd = lax.dot_general(kv_ref[listed[j]], qg, NT, preferred_element_type=jnp.float32)
            s = sd[:, :BS]
            if j > slots - STEP:
                s = jnp.where(j < count, s, -jnp.inf)
            s_s[j] = s
            d_s[j] = sd[:, BS:]
            top = s if top is None else jnp.maximum(top, s)
        top = jnp.max(top, axis=0, keepdims=True)
        norm = weighted = None
        for j in range(slots):
            e = jnp.exp(s_s[j] - top)
            s_s[j] = e
            ed = e * d_s[j]
            norm = e if norm is None else norm + e
            weighted = ed if weighted is None else weighted + ed
        inv = 1.0 / jnp.sum(norm, axis=0, keepdims=True)
        delta = jnp.sum(weighted, axis=0, keepdims=True) * inv
        dqt = None
        for j in range(0, slots, 2):
            ds_pair = []
            updates = []
            for k in (j, j + 1):
                p = s_s[k] * inv
                ds = (p * (d_s[k] - delta)).astype(jnp.bfloat16)
                ds_pair.append(ds)
                updates.append(dot(jnp.concatenate((ds, p.astype(jnp.bfloat16)), axis=1), qg))
            kt = jnp.concatenate((kt_s[listed[j]], kt_s[listed[j + 1]]), axis=1)
            term = dot(kt, jnp.concatenate(ds_pair, axis=0))
            dqt = term if dqt is None else dqt + term
            for k in (0, 1):
                dkv_s[listed[j + k]] += updates[k]
        out_ref[pl.ds(pl.multiple_of(b * BS, BS), BS), 2 * HD:] = dqt.T.astype(jnp.bfloat16)

    @pl.loop(0, block_count)
    def _(b):
        count = count_ref[b]
        for slots in range(STEP, KB + 1, STEP):
            @pl.when((count > slots - STEP) & (count <= slots))
            def _():
                one_block(b, count, slots)

    @pl.loop(0, block_count)
    def _(b):
        out_ref[pl.ds(pl.multiple_of(b * BS, BS), BS), :2 * HD] = dkv_s[b].astype(jnp.bfloat16)


def attention(qg, kv, block_row, count_row):
    nodes = qg.shape[0]
    block_count = nodes // BS
    vmem = pl.BlockSpec(memory_space=pltpu.VMEM)
    smem = pl.BlockSpec(memory_space=pltpu.SMEM)
    return pl.pallas_call(
        attend,
        out_shape=jax.ShapeDtypeStruct((nodes, 4 * HD), jnp.bfloat16),
        in_specs=[smem, smem, vmem, vmem],
        out_specs=vmem,
        scratch_shapes=[
            pltpu.VMEM((block_count, 2 * HD, BS), jnp.bfloat16),
            pltpu.VMEM((block_count, 2 * BS, 2 * HD), jnp.bfloat16),
            pltpu.VMEM((block_count, BS, 2 * HD), jnp.float32),
            pltpu.VMEM((KB, BS, BS), jnp.float32),
            pltpu.VMEM((KB, BS, BS), jnp.float32),
        ],
        compiler_params=pltpu.CompilerParams(vmem_limit_bytes=48 << 20),
        name="attend",
    )(block_row, count_row, qg.reshape(block_count, BS, 2 * HD), kv.reshape(block_count, BS, 2 * HD))


def collect(col_ref, g_ref, wq_ref, wk_ref, wv_ref, out_ref,
            pack, land, aq, ak, av, keep_s, give_s, got_s, pair_sem, send_sem, recv_sem):
    n, out_rows, _ = land.shape
    half = out_rows // 3
    graphs = out_ref.shape[0]
    heads = n // graphs
    nodes = g_ref.shape[0]
    me = lax.axis_index("head")
    side = lax.axis_index("tensor")
    barrier = pltpu.get_barrier_semaphore()
    pl.semaphore_signal(barrier, inc=1, device_id={"tensor": 1 - side}, device_id_type=MESH)

    @pl.loop(1, n)
    def _(k):
        pl.semaphore_signal(barrier, inc=1, device_id={"head": lax.rem(me + k, n)}, device_id_type=MESH)

    def make(peer, into):
        halves = []
        for u in range(2):
            start = pl.multiple_of((peer * 2 + u) * half, half)
            ids = lax.broadcasted_iota(jnp.int32, (half, nodes), 1)
            hot = jnp.where(ids == col_ref[pl.ds(start, half), :], 1.0, 0.0).astype(jnp.bfloat16)
            got = dot(hot, g_ref[...])
            into[u * half:(u + 1) * half] = got[:, :2 * HD].astype(jnp.bfloat16)
            halves.append(got[:, 2 * HD:])
        low = lax.broadcasted_iota(jnp.int32, (half, 2 * HD), 1) < HD
        into[2 * half:] = jnp.where(low, halves[0], halves[1]).astype(jnp.bfloat16)

    def copy_to(peer, slot):
        return pltpu.make_async_remote_copy(
            src_ref=pack.at[peer], dst_ref=land.at[slot],
            send_sem=send_sem.at[peer], recv_sem=recv_sem.at[slot],
            device_id={"head": peer}, device_id_type=MESH,
        )

    pl.semaphore_wait(barrier, n)

    @pl.loop(1, n)
    def _(k):
        peer = lax.rem(me + k, n)
        make(peer, pack.at[peer])
        copy_to(peer, me).start()

    make(me, land.at[me])

    @pl.loop(1, n)
    def _(k):
        source = lax.rem(me + n - k, n)
        copy_to(source, source).wait_recv()

    @pl.loop(0, graphs)
    def _(g):
        for h in range(heads):
            cols = slice(h * HD, (h + 1) * HD)
            slot = g * heads + h
            aq[:half, cols] = land[slot, 2 * half:, :HD]
            aq[half:, cols] = land[slot, 2 * half:, HD:]
            ak[:, cols] = land[slot, :2 * half, :HD]
            av[:, cols] = land[slot, :2 * half, HD:]

        def rows_at(part):
            rows = pl.ds(pl.multiple_of(part * half, half), half)
            total = lax.dot_general(aq[rows], wq_ref[...], NT, preferred_element_type=jnp.float32)
            total += lax.dot_general(ak[rows], wk_ref[...], NT, preferred_element_type=jnp.float32)
            total += lax.dot_general(av[rows], wv_ref[...], NT, preferred_element_type=jnp.float32)
            return total

        give_s[g] = rows_at(1 - side).astype(jnp.bfloat16)
        keep_s[g] = rows_at(side)

    pair = pltpu.make_async_remote_copy(
        src_ref=give_s, dst_ref=got_s, send_sem=pair_sem.at[0], recv_sem=pair_sem.at[1],
        device_id={"tensor": 1 - side}, device_id_type=MESH,
    )
    pair.start()
    pair.wait()
    out_ref[...] = (keep_s[...] + got_s[...].astype(jnp.float32)).astype(jnp.bfloat16)

    @pl.loop(1, n)
    def _(k):
        copy_to(lax.rem(me + k, n), me).wait_send()


def collecting(order, grads, w_query, w_key, w_value, graphs, n):
    nodes = order.shape[0]
    part_rows = nodes // n
    full, width = w_query.shape
    vmem = pl.BlockSpec(memory_space=pltpu.VMEM)
    chunks = pltpu.VMEM((n, part_rows * 3 // 2, 2 * HD), jnp.bfloat16)
    result = (graphs, part_rows // 2, full)
    return pl.pallas_call(
        collect,
        out_shape=jax.ShapeDtypeStruct(result, jnp.bfloat16),
        in_specs=[vmem] * 5,
        out_specs=vmem,
        scratch_shapes=[
            chunks, chunks,
            pltpu.VMEM((part_rows, width), jnp.bfloat16),
            pltpu.VMEM((part_rows, width), jnp.bfloat16),
            pltpu.VMEM((part_rows, width), jnp.bfloat16),
            pltpu.VMEM(result, jnp.float32),
            pltpu.VMEM(result, jnp.bfloat16),
            pltpu.VMEM(result, jnp.bfloat16),
            pltpu.SemaphoreType.DMA((2,)),
            pltpu.SemaphoreType.DMA((n,)),
            pltpu.SemaphoreType.DMA((n,)),
        ],
        compiler_params=pltpu.CompilerParams(
            vmem_limit_bytes=48 << 20, collective_id=1, has_side_effects=True
        ),
        name="collect",
    )(order.reshape(nodes, 1), grads, w_query, w_key, w_value)


def on_device(
    query, keys_in, values_in, grad_out, w_out, w_query, w_key, w_value, perm, blocks, counts
):
    local_rows, half_width = query.shape
    graphs, nodes = perm.shape
    half_heads = half_width // HD
    part_rows = local_rows // graphs
    n = nodes // part_rows
    graph = lax.axis_index("head") // half_heads
    order = lax.dynamic_index_in_dim(perm, graph, 0, keepdims=False)
    block_row = lax.dynamic_index_in_dim(blocks, graph, 0, keepdims=False)
    count_row = lax.dynamic_index_in_dim(counts, graph, 0, keepdims=False)
    by_graph = [
        member.reshape(part_rows, graphs, half_width).transpose(1, 0, 2).reshape(local_rows, half_width)
        for member in (query, keys_in, values_in, grad_out)
    ]
    qg, kv = spreading(order, *by_graph, w_out, n)
    grads = attention(qg, kv, block_row, count_row)
    total = collecting(order, grads, w_query, w_key, w_value, graphs, n)
    return total.transpose(1, 0, 2).reshape(local_rows // 2, -1)


def solution(mesh):
    return jax.shard_map(
        on_device,
        mesh=mesh,
        in_specs=(
            P(("groups", "head"), "tensor"),
            P(("groups", "head"), "tensor"),
            P(("groups", "head"), "tensor"),
            P(("groups", "head"), "tensor"),
            P("tensor", None),
            P(None, "tensor"),
            P(None, "tensor"),
            P(None, "tensor"),
            P("groups", None),
            P("groups", None, None),
            P("groups", None),
        ),
        out_specs=P(("groups", "head", "tensor"), None),
        check_vma=False,
    )
```

time: 193 us -> 154 us (0.80)
  the two profiles are of different devices: /device:TPU:0 before, /device:TPU:13 now
where the time goes in v2:
time: 154 us; the launch traced here: 153 us
  Pallas kernels  141 us (92%)
  local copies, waits for them, and re-layouts  12 us (8%)
    pallas_call x1, Pallas kernels, spreading(): pl.pallas_call(spread, out_shape=(half, half), in_specs=[vmem] * 6, out_s...  61.6 us
    pallas_call x1, Pallas kernels, collecting(): pl.pallas_call(collect, out_shape=jax.ShapeDtypeStruct(result, jnp.bfloat...  46.7 us
    pallas_call x1, Pallas kernels, attention(): pl.pallas_call(attend, out_shape=jax.ShapeDtypeStruct((nodes, 4 * HD), jn...  32.3 us
    unnamed x28, local copies, waits for them, and re-layouts  11.4 us

profile of v2, /device:TPU:13, one launch (start us, length us, event | category | flops | bytes accessed | tf_op | source)
XLA Modules:
  0.0 152.7 jit_solution(1082049311471481741)
XLA Ops:
  0.0 0.0 copy-start.11
  0.0 0.0 copy-start.1
  0.0 1.2 copy-done.1
  1.2 0.0 copy-start.5
  1.2 1.0 copy-done.5
  2.3 0.0 copy-start.6
  2.3 1.0 copy-done.6
  3.3 1.0 copy-done.7
  4.4 1.0 copy-done.8
  5.4 0.7 copy-done.9
  6.1 61.6 %spread.1 = (bf16[4096,128]{1,0:T(8,128)(2,1)S(1)}, bf16[4096,128]{1,0:T(8,128)(2,1)S(1)}) custom-call(s32[8,1,512]{2,1,0:T(1,128)S(1)} %bitcast.10, bf16[512,512]{1,0:T(8,128)(2,1)S(1)} %copy-done.5, bf16[512,512]{1,0:T(8,128)(2,1)S(1)} %copy-done.6, bf16[512,512]{1,0:T(8,128)(2,1)S(1)} %copy-done.7, bf16[512,512]{1,0:T(8,128)(2,1)S(1)} %copy-done.8, ...), custom_call_target="tpu_custom_call" | custom-call | tf_op jit(solution)/shard_map/spread/pallas_call | solution.py:119
  67.8 0.0 copy-done.12
  67.8 0.1 copy.13
  67.9 0.0 copy-done.11
  67.9 32.3 %attend.1.g_ref = bf16[4096,256]{1,0:T(8,128)(2,1)S(1)} custom-call(s32[32,12]{1,0:T(8,128)S(1)} %bitcast.12, s32[32]{0:T(128)S(1)} %bitcast.13, bf16[32,128,128]{2,1,0:T(8,128)(2,1)S(1)} %bitcast.8, bf16[32,128,128]{2,1,0:T(8,128)(2,1)S(1)} %bitcast.9), custom_call_target="tpu_custom_call" | custom-call | tf_op jit(solution)/shard_map/attend/pallas_call | solution.py:211
  100.2 0.0 copy-start
  100.2 1.3 copy-done
  101.5 0.0 copy-done.10
  101.5 0.6 copy.14.col_ref
  102.2 0.6 copy-done.2
  102.8 1.2 copy-done.3
  104.0 1.2 copy-done.4
  105.2 46.7 %collect.1 = bf16[1,256,1024]{2,1,0:T(8,128)(2,1)S(1)} custom-call(s32[4096,1]{1,0:T(8,128)S(1)} %copy.14.col_ref, bf16[4096,256]{1,0:T(8,128)(2,1)} %copy-done, bf16[1024,512]{1,0:T(8,128)(2,1)S(1)} %copy-done.2, bf16[1024,512]{1,0:T(8,128)(2,1)S(1)} %copy-done.3, bf16[1024,512]{1,0:T(8,128)(2,1)S(1)} %copy-done.4), custom_call_target="tpu_custom_call" | custom-call | tf_op jit(solution)/shard_map/collect/pallas_call | solution.py:318
  151.9 0.8 copy.16
  (8 shorter events, 0.0 us)
Async XLA Ops:
  0.0 67.9 %copy-start.11 = (s32[1,32]{1,0:T(1,128)S(1)}, s32[1,32]{1,0:T(1,128)}, u32[]{:S(2)}) copy-start(s32[1,32]{1,0:T(1,128)} %param.21) | copy-start | bytes 388
  0.0 1.2 copy-start.1
  1.2 1.0 copy-start.5
  2.3 1.0 copy-start.6
  3.3 1.0 copy-start.7
  4.4 1.0 copy-start.8
  5.4 0.7 copy-start.9
  6.1 61.6 %copy-start.12 = (s32[1,32,12]{1,0,2:T(1,128)S(1)}, s32[1,32,12]{1,0,2:T(1,128)}, u32[]{:S(2)}) copy-start(s32[1,32,12]{1,0,2:T(1,128)} %param.20) | copy-start | bytes 4612
  67.9 33.7 %copy-start.10 = (s32[1,4096]{1,0:T(1,128)S(1)}, s32[1,4096]{1,0:T(1,128)}, u32[]{:S(2)}) copy-start(s32[1,4096]{1,0:T(1,128)} %param.19) | copy-start | bytes 49156
  100.2 1.3 copy-start
  101.5 1.2 copy-start.2
  102.8 1.2 copy-start.3
  104.0 1.2 copy-start.4

commit v3 on v2

--- a/solution.py
+++ b/solution.py
@@ -9,7 +9,8 @@
 BS = 128
 KB = 12
 NT = (((1,), (1,)), ((), ()))
-STEP = 4
+STEP = 2
+VMEM_BYTES = 67043328
 TILE = 512
 MESH = pl.DeviceIdType.MESH
 
@@ -18,8 +19,12 @@
     return jnp.dot(a, b, preferred_element_type=jnp.float32)
 
 
-def spread(row_ref, q_ref, k_ref, v_ref, go_ref, w_ref, qg_out, kv_out,
-           grad_s, attn_s, kv_pack, qg_pack, kv_in, qg_in, acc_s, pair_sem, send_sem, recv_sem):
+def hop(i, n):
+    return n // 2 + (1 - 2 * lax.rem(i, 2)) * ((i + 1) // 2)
+
+
+def spread(row_ref, q_hbm, k_hbm, v_hbm, go_hbm, w_hbm, qg_out, kv_out,
+           q_ref, k_ref, v_ref, go_ref, w_ref, load_sem, grad_s, attn_s, kv_pack, qg_pack, kv_in, qg_in, acc_s, pair_sem, send_sem, recv_sem):
     n, part_rows, _ = kv_in.shape
     heads = q_ref.shape[1] // HD
     graphs = n // heads
@@ -27,12 +32,23 @@
     me = lax.axis_index("head")
     side = lax.axis_index("tensor")
     width = go_ref.shape[1]
+    loads = [
+        pltpu.make_async_copy(src, dst, load_sem.at[at])
+        for at, (src, dst) in enumerate(
+            ((k_hbm, k_ref), (v_hbm, v_ref), (go_hbm, go_ref), (q_hbm, q_ref), (w_hbm, w_ref))
+        )
+    ]
+    for load in loads:
+        load.start()
     barrier = pltpu.get_barrier_semaphore()
     pl.semaphore_signal(barrier, inc=1, device_id={"tensor": 1 - side}, device_id_type=MESH)
 
     @pl.loop(1, n)
     def _(k):
         pl.semaphore_signal(barrier, inc=1, device_id={"head": lax.rem(me + k, n)}, device_id_type=MESH)
+
+    loads[0].wait()
+    loads[1].wait()
 
     @pl.loop(0, graphs)
     def _(g):
@@ -41,8 +57,8 @@
             cols = slice(h * HD, (h + 1) * HD)
             kv_pack[g * heads + h, :, :HD] = k_ref[rows, cols]
             kv_pack[g * heads + h, :, HD:] = v_ref[rows, cols]
-            qg_pack[g * heads + h, :, :HD] = q_ref[rows, cols]
-
+
+    loads[2].wait()
     pl.semaphore_wait(barrier, n)
     pair = pltpu.make_async_remote_copy(
         src_ref=go_ref, dst_ref=grad_s, send_sem=pair_sem.at[0], recv_sem=pair_sem.at[1],
@@ -58,11 +74,13 @@
         )
 
     def send_all(which, pack, land):
-        @pl.loop(1, n)
-        def _(k):
-            copy_to(which, pack, land, lax.rem(me + k, n), me).start()
+        @pl.loop(0, n - 1)
+        def _(i):
+            copy_to(which, pack, land, lax.rem(me + hop(i, n), n), me).start()
 
     send_all(0, kv_pack, kv_in)
+    loads[3].wait()
+    loads[4].wait()
     near = pl.ds(pl.multiple_of(side * width, width), width)
     far = pl.ds(pl.multiple_of((1 - side) * width, width), width)
     attn_s[...] = lax.dot_general(go_ref[...], w_ref[:, near], NT, preferred_element_type=jnp.float32)
@@ -74,6 +92,7 @@
         rows = pl.ds(pl.multiple_of(g * part_rows, part_rows), part_rows)
         for h in range(heads):
             cols = slice(h * HD, (h + 1) * HD)
+            qg_pack[g * heads + h, :, :HD] = q_ref[rows, cols]
             qg_pack[g * heads + h, :, HD:] = attn_s[rows, cols].astype(jnp.bfloat16)
 
     send_all(1, qg_pack, qg_in)
@@ -92,9 +111,9 @@
 
         add(pack[me], me, True)
 
-        @pl.loop(1, n)
-        def _(k):
-            source = lax.rem(me + n - k, n)
+        @pl.loop(0, n - 1)
+        def _(i):
+            source = lax.rem(me + n - hop(i, n), n)
             copy_to(which, pack, land, source, source).wait_recv()
             add(land[source], source, False)
 
@@ -119,9 +138,15 @@
     return pl.pallas_call(
         spread,
         out_shape=(half, half),
-        in_specs=[vmem] * 6,
+        in_specs=[vmem] + [pl.BlockSpec(memory_space=pltpu.HBM)] * 5,
         out_specs=(vmem, vmem),
         scratch_shapes=[
+            pltpu.VMEM(query.shape, jnp.bfloat16),
+            pltpu.VMEM(query.shape, jnp.bfloat16),
+            pltpu.VMEM(query.shape, jnp.bfloat16),
+            pltpu.VMEM(grad_out.shape, jnp.bfloat16),
+            pltpu.VMEM(w_out.shape, jnp.bfloat16),
+            pltpu.SemaphoreType.DMA((5,)),
             pltpu.VMEM(grad_out.shape, jnp.bfloat16),
             pltpu.VMEM(query.shape, jnp.float32),
             chunks, chunks, chunks, chunks,
@@ -131,7 +156,7 @@
             pltpu.SemaphoreType.DMA((2, n)),
         ],
         compiler_params=pltpu.CompilerParams(
-            vmem_limit_bytes=48 << 20, collective_id=0, has_side_effects=True
+            vmem_limit_bytes=VMEM_BYTES, collective_id=0, has_side_effects=True
         ),
         name="spread",
     )(order.reshape(n, 1, part_rows), query, keys_in, values_in, grad_out, w_out)
@@ -220,13 +245,13 @@
             pltpu.VMEM((KB, BS, BS), jnp.float32),
             pltpu.VMEM((KB, BS, BS), jnp.float32),
         ],
-        compiler_params=pltpu.CompilerParams(vmem_limit_bytes=48 << 20),
+        compiler_params=pltpu.CompilerParams(vmem_limit_bytes=VMEM_BYTES),
         name="attend",
     )(block_row, count_row, qg.reshape(block_count, BS, 2 * HD), kv.reshape(block_count, BS, 2 * HD))
 
 
-def collect(col_ref, g_ref, wq_ref, wk_ref, wv_ref, out_ref,
-            pack, land, aq, ak, av, keep_s, give_s, got_s, pair_sem, send_sem, recv_sem):
+def collect(col_ref, g_ref, wq_hbm, wk_hbm, wv_hbm, out_ref,
+            wq_ref, wk_ref, wv_ref, load_sem, pack, land, aq, ak, av, keep_s, give_s, got_s, pair_sem, send_sem, recv_sem):
     n, out_rows, _ = land.shape
     half = out_rows // 3
     graphs = out_ref.shape[0]
@@ -234,6 +259,12 @@
     nodes = g_ref.shape[0]
     me = lax.axis_index("head")
     side = lax.axis_index("tensor")
+    loads = [
+        pltpu.make_async_copy(src, dst, load_sem.at[at])
+        for at, (src, dst) in enumerate(((wq_hbm, wq_ref), (wk_hbm, wk_ref), (wv_hbm, wv_ref)))
+    ]
+    for load in loads:
+        load.start()
     barrier = pltpu.get_barrier_semaphore()
     pl.semaphore_signal(barrier, inc=1, device_id={"tensor": 1 - side}, device_id_type=MESH)
 
@@ -260,11 +291,14 @@
             device_id={"head": peer}, device_id_type=MESH,
         )
 
+    opposite = lax.rem(me + n // 2, n)
+    make(opposite, pack.at[opposite])
     pl.semaphore_wait(barrier, n)
-
-    @pl.loop(1, n)
-    def _(k):
-        peer = lax.rem(me + k, n)
+    copy_to(opposite, me).start()
+
+    @pl.loop(1, n - 1)
+    def _(i):
+        peer = lax.rem(me + hop(i, n), n)
         make(peer, pack.at[peer])
         copy_to(peer, me).start()
 
@@ -274,32 +308,39 @@
     def _(k):
         source = lax.rem(me + n - k, n)
         copy_to(source, source).wait_recv()
+
+    for load in loads:
+        load.wait()
+
+    def rows_at(g, part):
+        rows = pl.ds(pl.multiple_of(part * half, half), half)
+        total = lax.dot_general(aq[g, rows], wq_ref[...], NT, preferred_element_type=jnp.float32)
+        total += lax.dot_general(ak[g, rows], wk_ref[...], NT, preferred_element_type=jnp.float32)
+        total += lax.dot_general(av[g, rows], wv_ref[...], NT, preferred_element_type=jnp.float32)
+        return total
 
     @pl.loop(0, graphs)
     def _(g):
         for h in range(heads):
             cols = slice(h * HD, (h + 1) * HD)
             slot = g * heads + h
-            aq[:half, cols] = land[slot, 2 * half:, :HD]
-            aq[half:, cols] = land[slot, 2 * half:, HD:]
-            ak[:, cols] = land[slot, :2 * half, :HD]
-            av[:, cols] = land[slot, :2 * half, HD:]
-
-        def rows_at(part):
-            rows = pl.ds(pl.multiple_of(part * half, half), half)
-            total = lax.dot_general(aq[rows], wq_ref[...], NT, preferred_element_type=jnp.float32)
-            total += lax.dot_general(ak[rows], wk_ref[...], NT, preferred_element_type=jnp.float32)
-            total += lax.dot_general(av[rows], wv_ref[...], NT, preferred_element_type=jnp.float32)
-            return total
-
-        give_s[g] = rows_at(1 - side).astype(jnp.bfloat16)
-        keep_s[g] = rows_at(side)
+            aq[g, :half, cols] = land[slot, 2 * half:, :HD]
+            aq[g, half:, cols] = land[slot, 2 * half:, HD:]
+            ak[g, :, cols] = land[slot, :2 * half, :HD]
+            av[g, :, cols] = land[slot, :2 * half, HD:]
+
+        give_s[g] = rows_at(g, 1 - side).astype(jnp.bfloat16)
 
     pair = pltpu.make_async_remote_copy(
         src_ref=give_s, dst_ref=got_s, send_sem=pair_sem.at[0], recv_sem=pair_sem.at[1],
         device_id={"tensor": 1 - side}, device_id_type=MESH,
     )
     pair.start()
+
+    @pl.loop(0, graphs)
+    def _(g):
+        keep_s[g] = rows_at(g, side)
+
     pair.wait()
     out_ref[...] = (keep_s[...] + got_s[...].astype(jnp.float32)).astype(jnp.bfloat16)
 
@@ -318,13 +359,17 @@
     return pl.pallas_call(
         collect,
         out_shape=jax.ShapeDtypeStruct(result, jnp.bfloat16),
-        in_specs=[vmem] * 5,
+        in_specs=[vmem] * 2 + [pl.BlockSpec(memory_space=pltpu.HBM)] * 3,
         out_specs=vmem,
         scratch_shapes=[
+            pltpu.VMEM(w_query.shape, jnp.bfloat16),
+            pltpu.VMEM(w_query.shape, jnp.bfloat16),
+            pltpu.VMEM(w_query.shape, jnp.bfloat16),
+            pltpu.SemaphoreType.DMA((3,)),
             chunks, chunks,
-            pltpu.VMEM((part_rows, width), jnp.bfloat16),
-            pltpu.VMEM((part_rows, width), jnp.bfloat16),
-            pltpu.VMEM((part_rows, width), jnp.bfloat16),
+            pltpu.VMEM((graphs, part_rows, width), jnp.bfloat16),
+            pltpu.VMEM((graphs, part_rows, width), jnp.bfloat16),
+            pltpu.VMEM((graphs, part_rows, width), jnp.bfloat16),
             pltpu.VMEM(result, jnp.float32),
             pltpu.VMEM(result, jnp.bfloat16),
             pltpu.VMEM(result, jnp.bfloat16),
@@ -333,7 +378,7 @@
             pltpu.SemaphoreType.DMA((n,)),
         ],
         compiler_params=pltpu.CompilerParams(
-            vmem_limit_bytes=48 << 20, collective_id=1, has_side_effects=True
+            vmem_limit_bytes=VMEM_BYTES, collective_id=1, has_side_effects=True
         ),
         name="collect",
     )(order.reshape(nodes, 1), grads, w_query, w_key, w_value)

time: 154 us -> 150 us (0.974)
  local copies, waits for them, and re-layouts: 12 us -> 5.91 us
  Pallas kernels: 141 us -> 144 us
    unnamed x28 -> x2, local copies, waits for them, and re-layouts: 11.4 us -> 3.25 us
    pallas_call x1, Pallas kernels: 32.3 us -> 35.5 us  [attention(): pl.pallas_call(attend, out_shape=jax.ShapeDtypeStruct((nodes, 4 * HD), jn...]
    reshape x1, local copies, waits for them, and re-layouts: 0.64 us -> 2.67 us  [collecting(): order.reshape(nodes, 1)]
    pallas_call x1, Pallas kernels: 46.7 us -> 44.8 us  [collecting(): pl.pallas_call(collect, out_shape=jax.ShapeDtypeStruct(result, jnp.bfloat...]
    pallas_call x1, Pallas kernels: 61.6 us -> 63.4 us  [spreading(): pl.pallas_call(spread, out_shape=(half, half), in_specs=[vmem] + [pl.Bloc...]
where the time goes in v3:
time: 150 us
  Pallas kernels  144 us (96%)
  local copies, waits for them, and re-layouts  5.91 us (4%)
    pallas_call x1, Pallas kernels, spreading(): pl.pallas_call(spread, out_shape=(half, half), in_specs=[vmem] + [pl.Bloc...  63.4 us
    pallas_call x1, Pallas kernels, collecting(): pl.pallas_call(collect, out_shape=jax.ShapeDtypeStruct(result, jnp.bfloat...  44.8 us
    pallas_call x1, Pallas kernels, attention(): pl.pallas_call(attend, out_shape=jax.ShapeDtypeStruct((nodes, 4 * HD), jn...  35.5 us
    unnamed x2, local copies, waits for them, and re-layouts  3.25 us

profile of v3, /device:TPU:13, one launch (start us, length us, event | category | flops | bytes accessed | tf_op | source)
XLA Modules:
  0.0 149.7 jit_solution(4518726221255392548)
XLA Ops:
  0.0 63.4 %spread.1 = (bf16[4096,128]{1,0:T(8,128)(2,1)}, bf16[4096,128]{1,0:T(8,128)(2,1)}) custom-call(s32[8,1,512]{2,1,0:T(1,128)} %bitcast.10, bf16[512,512]{1,0:T(8,128)(2,1)} %q_hbm.1, bf16[512,512]{1,0:T(8,128)(2,1)} %k_hbm.1, bf16[512,512]{1,0:T(8,128)(2,1)} %v_hbm.1, bf16[512,512]{1,0:T(8,128)(2,1)} %go_hbm.1, bf16[512,1024]{1,0:T(8,128)(2,1)} %w_hbm.1), custom_call_target="tpu_custom_call" | custom-call | tf_op jit(solution)/shard_map/spread/pallas_call | solution.py:138
  63.4 1.4 copy.13
  64.8 35.5 %attend.1.g_ref = bf16[4096,256]{1,0:T(8,128)(2,1)} custom-call(s32[32,12]{1,0:T(8,128)} %bitcast.12, s32[32]{0:T(128)} %bitcast.13, bf16[32,128,128]{2,1,0:T(8,128)(2,1)} %bitcast.8, bf16[32,128,128]{2,1,0:T(8,128)(2,1)} %bitcast.9), custom_call_target="tpu_custom_call" | custom-call | tf_op jit(solution)/shard_map/attend/pallas_call | solution.py:236
  100.3 2.7 %copy.14.col_ref = s32[4096,1]{1,0:T(8,128)} copy(s32[4096,1]{0,1:T(1,128)} %bitcast.11) | data formatting | bytes 32768 | tf_op jit(solution)/shard_map/reshape | solution.py:384
  102.9 44.8 %collect.1 = bf16[1,256,1024]{2,1,0:T(8,128)(2,1)} custom-call(s32[4096,1]{1,0:T(8,128)} %copy.14.col_ref, bf16[4096,256]{1,0:T(8,128)(2,1)} %attend.1.g_ref, bf16[1024,512]{1,0:T(8,128)(2,1)} %wq_hbm.1, bf16[1024,512]{1,0:T(8,128)(2,1)} %wk_hbm.1, bf16[1024,512]{1,0:T(8,128)(2,1)} %wv_hbm.1), custom_call_target="tpu_custom_call" | custom-call | tf_op jit(solution)/shard_map/collect/pallas_call | solution.py:359
  147.8 1.9 %copy.16 = bf16[256,1024]{1,0:T(8,128)(2,1)} copy(bf16[256,1024]{1,0:T(8,128)(2,1)} %bitcast.7) | data formatting | bytes 1048576
